TPU v7x, 32 devices: a whole 2x2x4 slice. The times are simulated.
32 devices in a mesh: dp: 2 (over x), tm: 4 (over z), space: 4 (over y, core).
Axes of the slice: x: 2, y: 2, z: 4, core: 2. Of those that a mesh axis runs over, the one named last changes fastest.
Arguments:
- latent: bfloat16 [2, 12, 8, 104, 384], P('dp', 'tm', 'space'), may hold values from -16 to 16
- attn_gain: float32 [384], replicated, may hold values from 0.5 to 1.5
- w_query: bfloat16 [384, 384], replicated, may hold values from -1 to 1
- w_key: bfloat16 [384, 384], replicated, may hold values from -1 to 1
- w_value: bfloat16 [384, 384], replicated, may hold values from -0.3125 to 0.3125
- w_out: bfloat16 [384, 384], replicated, may hold values from -1.25 to 1.25
- conv_gain_first: float32 [384], replicated, may hold values from 0.5 to 1.5
- conv_first: bfloat16 [3, 3, 3, 384, 384], replicated, may hold values from -0.0625 to 0.0625
- conv_gain_second: float32 [384], replicated, may hold values from 0.5 to 1.5
- conv_second: bfloat16 [3, 3, 3, 384, 384], replicated, may hold values from -0.0625 to 0.0625
- student_in: bfloat16 [384, 384], replicated, may hold values from -0.3125 to 0.3125
- student_out: bfloat16 [384, 384], replicated, may hold values from -0.3125 to 0.3125
Outputs:
- teacher_out: bfloat16 [2, 12, 8, 104, 384], P('dp', 'tm', 'space')
- grad_in: float32 [384, 384], replicated
- grad_out: float32 [384, 384], replicated
All inputs are finite; a program needn't handle non-finite values.
Results may differ from a plain program's by a relative error of at most 0.007.
Values may be sent and summed in bfloat16 or wider, within the bound.
No kernel may reach another device: no remote copies, remote signals or barrier semaphores. Data moves between devices by JAX's collectives and lax.ppermute only.
A program may use at most 128 MiB of HBM per device.

v0:
```python
import jax
import jax.numpy as jnp
from jax import lax
from jax.sharding import PartitionSpec as P


def from_behind(value, axis, by):
    count = lax.axis_size(axis)
    pairs = [(i, i + by) for i in range(count) if 0 <= i + by < count]
    return lax.ppermute(value, axis, pairs)


def extended_2(block, sides, width):
    for axis, dim in sides:
        count = lax.axis_size(axis)
        forward = [(i, i + 1) for i in range(count - 1)]
        backward = [(target, source) for source, target in forward]
        low = lax.ppermute(
            lax.slice_in_dim(block, block.shape[dim] - width, None, axis=dim), axis, forward
        )
        high = lax.ppermute(lax.slice_in_dim(block, 0, width, axis=dim), axis, backward)
        block = jnp.concatenate([low, block, high], axis=dim)
    return block


def root_norm(values, gain):
    return values * lax.rsqrt(jnp.mean(values * values, axis=-1, keepdims=True) + 1e-06) * gain


def attend(queries, all_keys, all_values, scale):
    scores = (
        jnp.einsum("fqc,fkc->fqk", queries, all_keys, preferred_element_type=jnp.float32) * scale
    )
    maxima = jnp.max(scores, axis=-1, keepdims=True)
    expos = jnp.exp(scores - maxima)
    totals = jnp.sum(expos, axis=-1, keepdims=True)
    weights = expos.astype(jnp.bfloat16)
    summed = jnp.einsum("fqk,fkc->fqc", weights, all_values, preferred_element_type=jnp.float32)
    return (summed / totals).astype(jnp.bfloat16)


def causal_conv(activation, weight):
    frame_count, row_count, column_count, channels = activation.shape
    earlier = from_behind(activation[frame_count - 2 :], "tm", 1)
    extended = jnp.concatenate([earlier, activation], axis=0)
    extended = extended_2(extended, (("space", 1),), 1)
    extended = jnp.pad(extended, ((0, 0), (0, 0), (1, 1), (0, 0)))
    total = jnp.zeros((frame_count * row_count * column_count, channels), jnp.float32)
    for tap_time in range(3):
        for tap_row in range(3):
            for tap_col in range(3):
                window = extended[
                    tap_time : tap_time + frame_count,
                    tap_row : tap_row + row_count,
                    tap_col : tap_col + column_count,
                ]
                total = total + jnp.dot(
                    window.reshape(-1, channels),
                    weight[tap_time, tap_row, tap_col],
                    preferred_element_type=jnp.float32,
                )
    return total


def shards(
    latent,
    attn_gain,
    w_query,
    w_key,
    w_value,
    w_out,
    conv_gain_first,
    conv_first,
    conv_gain_second,
    conv_second,
    student_in,
    student_out,
):
    frames = latent[0]
    frame_count, row_count, column_count, channels = frames.shape
    per_frame = row_count * column_count
    tokens_local = frames.reshape(-1, channels)
    inputs_wide = tokens_local.astype(jnp.float32)
    normed = root_norm(inputs_wide, attn_gain).astype(jnp.bfloat16)
    queries = (
        jnp.dot(normed, w_query, preferred_element_type=jnp.float32)
        .astype(jnp.bfloat16)
        .reshape(frame_count, per_frame, channels)
    )
    scale = channels ** (-0.5)
    piece = lax.all_gather(
        normed.reshape(frame_count, per_frame, channels), "space", axis=1, tiled=True
    )
    rows_flat = piece.reshape(-1, channels)
    piece_keys = jnp.dot(rows_flat, w_key, preferred_element_type=jnp.float32).astype(jnp.bfloat16)
    piece_values = jnp.dot(rows_flat, w_value, preferred_element_type=jnp.float32).astype(
        jnp.bfloat16
    )
    stacked = jnp.stack([piece_keys.reshape(piece.shape), piece_values.reshape(piece.shape)])
    mixed = attend(queries, stacked[0], stacked[1], scale)
    attention_out = jnp.dot(mixed.reshape(-1, channels), w_out, preferred_element_type=jnp.float32)
    mid = (inputs_wide + attention_out).astype(jnp.bfloat16)
    mid_wide = mid.astype(jnp.float32)
    first_act = jax.nn.silu(root_norm(mid_wide, conv_gain_first)).astype(jnp.bfloat16)
    first_conv = causal_conv(
        first_act.reshape(frame_count, row_count, column_count, channels), conv_first
    )
    second_act = jax.nn.silu(root_norm(first_conv, conv_gain_second)).astype(jnp.bfloat16)
    second_conv = causal_conv(
        second_act.reshape(frame_count, row_count, column_count, channels), conv_second
    )
    teacher = (mid_wide + second_conv).astype(jnp.bfloat16)
    student_pre = jnp.dot(tokens_local, student_in, preferred_element_type=jnp.float32)
    student_hidden = jax.nn.silu(student_pre).astype(jnp.bfloat16)
    predicted = inputs_wide + jnp.dot(
        student_hidden, student_out, preferred_element_type=jnp.float32
    )
    error = predicted - teacher.astype(jnp.float32)
    token_total = (
        frame_count * per_frame * lax.axis_size("dp") * lax.axis_size("tm") * lax.axis_size("space")
    )
    signal = (error * lax.rsqrt(error * error + 0.0625) * token_total ** (-0.5)).astype(
        jnp.bfloat16
    )
    over_tokens = (((0,), (0,)), ((), ()))
    local_out = lax.dot_general(
        student_hidden, signal, over_tokens, preferred_element_type=jnp.float32
    )
    back = lax.dot_general(
        signal, student_out, (((1,), (1,)), ((), ())), preferred_element_type=jnp.float32
    )
    logistic = jax.nn.sigmoid(student_pre)
    back_pre = (back * logistic * (1.0 + student_pre * (1.0 - logistic))).astype(jnp.bfloat16)
    local_in = lax.dot_general(
        tokens_local, back_pre, over_tokens, preferred_element_type=jnp.float32
    )
    grad_in, grad_out = lax.psum((local_in, local_out), ("dp", "tm", "space"))
    return (teacher.reshape(latent.shape), grad_in, grad_out)


def solution(mesh):
    return jax.shard_map(
        shards,
        mesh=mesh,
        in_specs=(
            P("dp", "tm", "space", None, None),
            P(),
            P(),
            P(),
            P(),
            P(),
            P(),
            P(),
            P(),
            P(),
            P(),
            P(),
        ),
        out_specs=(P("dp", "tm", "space", None, None), P(), P()),
        check_vma=False,
    )
```

profile of v0, /device:TPU:0, one launch (start us, length us, event | category | flops | bytes accessed | tf_op | source)
XLA Modules:
  0.0 266.9 jit_solution(10811238338962035714)
XLA Ops:
  7.2 1.2 multiply_reduce_fusion.2
  8.6 2.0 multiply_convert_fusion.3
  10.7 1.7 convolution_convert_fusion.2
  12.4 22.6 %all-gather.2.cloned.1.call-done = bf16[3,832,384]{2,1,0:T(8,128)(2,1)} async-done(((bf16[3,208,384]{2,1,0:T(8,128)(2,1)}), bf16[3,832,384]{2,1,0:T(8,128)(2,1)}) %all-gather.2.cloned.1.call-update) | async-done | bytes 1916944 | tf_op jit(solution)/shard_map/all_gather | solution.py:91
  35.0 3.0 %convolution_convert_fusion.1 = bf16[2496,384]{1,0:T(8,128)(2,1)S(1)} fusion(bf16[2496,384]{1,0:T(8,128)(2,1)} %bitcast.304, bf16[384,384]{1,0:T(8,128)(2,1)S(1)} %copy-done), kind=kOutput, calls=%fused_computation.3 | convolution fusion | flops 737058816 | bytes 4128768 | tf_op jit(solution)/shard_map/dot_general | solution.py:95
  38.1 1.3 convolution_convert_fusion
  39.4 1.0 multiply_reduce_fusion
  40.4 0.6 fusion.1
  41.1 1.0 fusion.47
  42.1 0.6 fusion.54
  43.1 3.4 %collective-permute-start = (bf16[2,2,104,384]{3,2,1,0:T(8,128)(2,1)S(1)}, bf16[2,2,104,384]{3,2,1,0:T(8,128)(2,1)S(1)}, u32[]{:S(2)}, u32[]{:S(2)}) collective-permute-start(bf16[2,2,104,384]{3,2,1,0:T(8,128)(2,1)S(1)} %bitcast.381), channel_id=1, source_target_pairs={{0,4},{4,8},{8,12},{1,5},{5,9},{9,13},{2,6},{6,10},{10,14},{3,7},{... | collective-permute-start | bytes 958472 | tf_op jit(solution)/shard_map/ppermute | solution.py:10
  47.1 6.6 %collective-permute-done = bf16[2,2,104,384]{3,2,1,0:T(8,128)(2,1)S(1)} collective-permute-done((bf16[2,2,104,384]{3,2,1,0:T(8,128)(2,1)S(1)}, bf16[2,2,104,384]{3,2,1,0:T(8,128)(2,1)S(1)}, u32[]{:S(2)}, u32[]{:S(2)}) %collective-permute-start) | collective-permute-done | bytes 319520 | tf_op jit(solution)/shard_map/ppermute | solution.py:10
  53.8 1.3 collective-permute-start.1
  55.1 1.5 collective-permute-start.2
  57.7 1.8 collective-permute-done.2
  59.5 0.7 fusion.10
  60.2 2.6 fusion.226
  63.8 0.5 fusion.163
  69.9 0.5 fusion.133
  71.9 0.7 fusion.44
  72.6 0.5 fusion.42
  73.1 0.7 fusion.40
  73.8 0.5 fusion.35
  74.3 0.6 fusion.33
  75.0 0.5 fusion.31
  75.5 0.6 multiply_reduce_fusion.1
  76.5 4.7 %collective-permute-start.3 = (bf16[2,2,104,384]{3,2,1,0:T(8,128)(2,1)S(1)}, bf16[2,2,104,384]{3,2,1,0:T(8,128)(2,1)S(1)}, u32[]{:S(2)}, u32[]{:S(2)}) collective-permute-start(bf16[2,2,104,384]{3,2,1,0:T(8,128)(2,1)S(1)} %bitcast.380), channel_id=1, source_target_pairs={{0,4},{4,8},{8,12},{1,5},{5,9},{9,13},{2,6},{6,10},{10,14},{3,7},{... | collective-permute-start | bytes 958472 | tf_op jit(solution)/shard_map/ppermute | solution.py:10
  81.2 0.6 multiply_convert_fusion.1
  82.3 3.3 %collective-permute-done.3 = bf16[2,2,104,384]{3,2,1,0:T(8,128)(2,1)S(1)} collective-permute-done((bf16[2,2,104,384]{3,2,1,0:T(8,128)(2,1)S(1)}, bf16[2,2,104,384]{3,2,1,0:T(8,128)(2,1)S(1)}, u32[]{:S(2)}, u32[]{:S(2)}) %collective-permute-start.3) | collective-permute-done | bytes 319520 | tf_op jit(solution)/shard_map/ppermute | solution.py:10
  85.8 7.1 %collective-permute-start.4 = (bf16[5,1,104,384]{3,2,1,0:T(8,128)(2,1)S(1)}, bf16[5,1,104,384]{3,2,1,0:T(8,128)(2,1)S(1)}, u32[]{:S(2)}, u32[]{:S(2)}) collective-permute-start(bf16[5,1,104,384]{3,2,1,0:T(8,128)(2,1)S(1)} %get-tuple-element.60), channel_id=1, source_target_pairs={{0,1},{1,2},{2,3},{4,5},{5,6},{6,7},{8,9},{9,10},{10,11},{12,13},{... | collective-permute-start | bytes 1198088 | tf_op jit(solution)/shard_map/ppermute | solution.py:18
  92.9 1.3 collective-permute-start.5
  95.3 1.4 collective-permute-done.5
  96.7 0.7 select_maximum_fusion
  97.4 2.8 %fusion.225 = (bf16[3,2,104,384]{3,2,1,0:T(8,128)(2,1)S(1)}, bf16[3,2,104,384]{3,2,1,0:T(8,128)(2,1)S(1)}, bf16[3,2,104,384]{3,2,1,0:T(8,128)(2,1)S(1)}, bf16[3,...) fusion(bf16[5,4,106,384]{3,2,1,0:T(8,128)(2,1)S(1)} %select_max, ...), kind=kLoop, calls=%fused_computation.283 | loop fusion | bytes 17252352 | tf_op jit(solution)/shard_map/slice | solution.py:52
  104.7 0.5 fusion.93
  109.3 0.8 fusion.29
  110.0 0.5 fusion.27
  110.6 0.7 fusion.25
  111.2 0.6 fusion.20
  111.8 0.6 fusion.18
  112.4 0.5 fusion.16
  112.9 0.5 fusion.48
  113.5 0.7 multiply_convert_fusion
  114.1 1.3 fusion.231
  115.4 1.8 convolution_bitcast_fusion
  117.3 138.7 %all-reduce.5.cloned.1.call-done = (f32[384,384]{0,1:T(8,128)}, f32[384,384]{1,0:T(8,128)}) async-done(((f32[384,384]{0,1:T(8,128)}, f32[384,384]{1,0:T(8,128)}), (f32[384,384]{0,1:T(8,128)}, f32[384,384]{1,0:T(8,128)})) %all-reduce.5.cloned.1.call-update) | async-done | bytes 1179664 | tf_op jit(solution)/shard_map/psum | solution.py:137
  256.0 2.1 copy.15
  258.1 1.9 copy.18
  (93 shorter events, 21.1 us)
Async XLA Ops:
  7.2 27.9 %copy-start = (bf16[384,384]{1,0:T(8,128)(2,1)S(1)}, bf16[384,384]{1,0:T(8,128)(2,1)}, u32[]{:S(2)}) copy-start(bf16[384,384]{1,0:T(8,128)(2,1)} %param.15) | copy-start | bytes 884740
  7.2 27.9 %all-gather.2.cloned.1.call-start = ((), (), s32[]{:S(2)}) async-start(), calls=%async_computation | async-start | bytes 2396160 | tf_op jit(solution)/shard_map/all_gather | solution.py:91
  10.6 245.4 %all-reduce.5.cloned.1.call-start = ((), (), s32[]{:S(2)}) async-start(), calls=%async_computation.1 | async-start | bytes 2359296 | tf_op jit(solution)/shard_map/psum | solution.py:137
  12.4 25.6 %copy-start.5 = (bf16[384,384]{1,0:T(8,128)(2,1)S(1)}, bf16[384,384]{1,0:T(8,128)(2,1)}, u32[]{:S(2)}) copy-start(bf16[384,384]{1,0:T(8,128)(2,1)} %param.16) | copy-start | bytes 884740
  35.0 3.0 %copy-start.2 = (bf16[3,832,384]{2,1,0:T(8,128)(2,1)S(1)}, bf16[3,832,384]{2,1,0:T(8,128)(2,1)}, u32[]{:S(2)}) copy-start(bf16[3,832,384]{2,1,0:T(8,128)(2,1)} %all-gather.2.cloned.1.call-done) | copy-start | bytes 5750788
  39.4 7.2 %slice-start = ((s8[7962624]{0:T(1024)(128)(4,1)}), s8[4194304]{0:T(1024)(128)(4,1)S(1)}, s32[]{:S(2)}) async-start(s8[7962624]{0:T(1024)(128)(4,1)} %bitcast.315), calls=%async_computation.2 | async-start | bytes 8388608
  41.0 1.0 copy-start.3
  41.0 1.1 copy-start.8
  41.0 1.7 copy-start.6
  41.1 5.5 %slice-start.1 = ((s8[7962624]{0:T(1024)(128)(4,1)}), s8[3768320]{0:T(1024)(128)(4,1)S(1)}, s32[]{:S(2)}) async-start(s8[7962624]{0:T(1024)(128)(4,1)} %bitcast.315), calls=%async_computation.3 | async-start | bytes 7536640
  43.1 10.6 %collective-permute-start = (bf16[2,2,104,384]{3,2,1,0:T(8,128)(2,1)S(1)}, bf16[2,2,104,384]{3,2,1,0:T(8,128)(2,1)S(1)}, u32[]{:S(2)}, u32[]{:S(2)}) collective-permute-start(bf16[2,2,104,384]{3,2,1,0:T(8,128)(2,1)S(1)} %bitcast.381), channel_id=1, source_target_pairs={{0,4},{4,8},{8,12},{1,5},{5,9},{9,13},{2,6},{6,10},{10,14},{3,7},{... | collective-permute-start | bytes 958472 | tf_op jit(solution)/shard_map/ppermute | solution.py:10
  53.8 3.9 %collective-permute-start.1 = (bf16[5,1,104,384]{3,2,1,0:T(8,128)(2,1)S(1)}, bf16[5,1,104,384]{3,2,1,0:T(8,128)(2,1)S(1)}, u32[]{:S(2)}, u32[]{:S(2)}) collective-permute-start(bf16[5,1,104,384]{3,2,1,0:T(8,128)(2,1)S(1)} %get-tuple-element.66), channel_id=1, source_target_pairs={{0,1},{1,2},{2,3},{4,5},{5,6},{6,7},{8,9},{9,10},{10,11},{12,13},{... | collective-permute-start | bytes 1198088 | tf_op jit(solution)/shard_map/ppermute | solution.py:18
  55.1 4.4 %collective-permute-start.2 = (bf16[5,1,104,384]{3,2,1,0:T(8,128)(2,1)S(1)}, bf16[5,1,104,384]{3,2,1,0:T(8,128)(2,1)S(1)}, u32[]{:S(2)}, u32[]{:S(2)}) collective-permute-start(bf16[5,1,104,384]{3,2,1,0:T(8,128)(2,1)S(1)} %get-tuple-element.67), channel_id=1, source_target_pairs={{1,0},{2,1},{3,2},{5,4},{6,5},{7,6},{9,8},{10,9},{11,10},{13,12},{... | collective-permute-start | bytes 1198088 | tf_op jit(solution)/shard_map/ppermute | solution.py:21
  74.9 1.2 copy-start.7
  74.9 6.2 %copy-start.9 = (bf16[384,384]{1,0:T(8,128)(2,1)S(1)}, bf16[384,384]{1,0:T(8,128)(2,1)}, u32[]{:S(2)}) copy-start(bf16[384,384]{1,0:T(8,128)(2,1)} %param.22) | copy-start | bytes 884740
  74.9 6.8 %slice-start.2 = ((s8[7962624]{0:T(1024)(128)(4,1)}), s8[4194304]{0:T(1024)(128)(4,1)S(1)}, s32[]{:S(2)}) async-start(s8[7962624]{0:T(1024)(128)(4,1)} %bitcast.317), calls=%async_computation.4 | async-start | bytes 8388608
  75.5 6.3 %slice-start.3 = ((s8[7962624]{0:T(1024)(128)(4,1)}), s8[3768320]{0:T(1024)(128)(4,1)S(1)}, s32[]{:S(2)}) async-start(s8[7962624]{0:T(1024)(128)(4,1)} %bitcast.317), calls=%async_computation.5 | async-start | bytes 7536640
  76.5 9.1 %collective-permute-start.3 = (bf16[2,2,104,384]{3,2,1,0:T(8,128)(2,1)S(1)}, bf16[2,2,104,384]{3,2,1,0:T(8,128)(2,1)S(1)}, u32[]{:S(2)}, u32[]{:S(2)}) collective-permute-start(bf16[2,2,104,384]{3,2,1,0:T(8,128)(2,1)S(1)} %bitcast.380), channel_id=1, source_target_pairs={{0,4},{4,8},{8,12},{1,5},{5,9},{9,13},{2,6},{6,10},{10,14},{3,7},{... | collective-permute-start | bytes 958472 | tf_op jit(solution)/shard_map/ppermute | solution.py:10
  85.8 9.5 %collective-permute-start.4 = (bf16[5,1,104,384]{3,2,1,0:T(8,128)(2,1)S(1)}, bf16[5,1,104,384]{3,2,1,0:T(8,128)(2,1)S(1)}, u32[]{:S(2)}, u32[]{:S(2)}) collective-permute-start(bf16[5,1,104,384]{3,2,1,0:T(8,128)(2,1)S(1)} %get-tuple-element.60), channel_id=1, source_target_pairs={{0,1},{1,2},{2,3},{4,5},{5,6},{6,7},{8,9},{9,10},{10,11},{12,13},{... | collective-permute-start | bytes 1198088 | tf_op jit(solution)/shard_map/ppermute | solution.py:18
  92.9 3.8 %collective-permute-start.5 = (bf16[5,1,104,384]{3,2,1,0:T(8,128)(2,1)S(1)}, bf16[5,1,104,384]{3,2,1,0:T(8,128)(2,1)S(1)}, u32[]{:S(2)}, u32[]{:S(2)}) collective-permute-start(bf16[5,1,104,384]{3,2,1,0:T(8,128)(2,1)S(1)} %get-tuple-element.61), channel_id=1, source_target_pairs={{1,0},{2,1},{3,2},{5,4},{6,5},{7,6},{9,8},{10,9},{11,10},{13,12},{... | collective-permute-start | bytes 1198088 | tf_op jit(solution)/shard_map/ppermute | solution.py:21
  112.4 1.1 copy-start.10
  113.4 3.8 %copy-start.4 = (bf16[624,384]{1,0:T(8,128)(2,1)}, bf16[624,384]{1,0:T(8,128)(2,1)S(1)}, u32[]{:S(2)}) copy-start(bf16[624,384]{1,0:T(8,128)(2,1)S(1)} %fusion.48) | copy-start | bytes 1437700
  115.4 144.6 %copy-start.1 = (bf16[384,384]{1,0:T(8,128)(2,1)S(1)}, bf16[384,384]{1,0:T(8,128)(2,1)}, u32[]{:S(2)}) copy-start(bf16[384,384]{1,0:T(8,128)(2,1)} %param.15) | copy-start | bytes 884740
Sparse Core Ops, SparseCore 0:
  10.7 24.2 all-gather.1
  117.4 138.5 all-reduce.4
where the time goes:
time: 267 us
  waiting for transfers between devices  174 us (65%)
  matrix products  41 us (15%)
  starting transfers between devices  19.3 us (7%)
  between operations  14.7 us (6%)
  local copies, waits for them, and re-layouts  10.3 us (4%)
  other arithmetic  6.98 us (3%)
    psum x1, waiting for transfers between devices, shards(): grad_in, grad_out = lax.psum((local_in, local_out), ('dp', 'tm', 'space'))  139 us
    dot_general x54, matrix products, causal_conv(): jnp.dot(window.reshape(-1, channels), weight[tap_time, tap_row, tap_col],...  28.1 us
    all_gather x1, waiting for transfers between devices, shards(): lax.all_gather(normed.reshape(frame_count, per_frame, channels), 'space',...  22.6 us
    ppermute x2, waiting for transfers between devices, from_behind(): return lax.ppermute(value, axis, pairs)  9.94 us
    ppermute x2, starting transfers between devices, extended_2(): lax.ppermute(lax.slice_in_dim(block, block.shape[dim] - width, None, axis...  8.42 us
    ppermute x2, starting transfers between devices, from_behind(): return lax.ppermute(value, axis, pairs)  8.08 us
    slice x5, local copies, waits for them, and re-layouts, causal_conv(): extended[tap_time:tap_time + frame_count, tap_row:tap_row + row_count, ta...  5.87 us
  transfers between devices with their start and end apart: 8, of which 6 were waited for; matrix products, arithmetic and copies ran while one was open for 2% of the time, Pallas kernels for 0%

commit v1 on v0

--- a/solution.py
+++ b/solution.py
@@ -2,6 +2,18 @@
 import jax.numpy as jnp
 from jax import lax
 from jax.sharding import PartitionSpec as P
+
+
+def doubled_up(x, axis, dim):
+    ways, here = (lax.axis_size(axis), lax.axis_index(axis))
+    grown, reach = (x, 1)
+    while reach < ways:
+        theirs = lax.ppermute(grown, axis, [(d, d ^ reach) for d in range(ways)])
+        mine_first = jnp.concatenate([grown, theirs], axis=dim)
+        theirs_first = jnp.concatenate([theirs, grown], axis=dim)
+        grown = jnp.where(here & reach == 0, mine_first, theirs_first)
+        reach = 2 * reach
+    return grown
 
 
 def from_behind(value, axis, by):
@@ -88,9 +100,7 @@
         .reshape(frame_count, per_frame, channels)
     )
     scale = channels ** (-0.5)
-    piece = lax.all_gather(
-        normed.reshape(frame_count, per_frame, channels), "space", axis=1, tiled=True
-    )
+    piece = doubled_up(normed.reshape(frame_count, per_frame, channels), "space", 1)
     rows_flat = piece.reshape(-1, channels)
     piece_keys = jnp.dot(rows_flat, w_key, preferred_element_type=jnp.float32).astype(jnp.bfloat16)
     piece_values = jnp.dot(rows_flat, w_value, preferred_element_type=jnp.float32).astype(

time: 267 us -> 268 us (level)
  starting transfers between devices: 19.3 us -> 23.1 us
    all_gather x1 -> x0, waiting for transfers between devices: 22.6 us -> none  [shards(): lax.all_gather(normed.reshape(frame_count, per_frame, channels), 'space',...]
    ppermute x0 -> x2, waiting for transfers between devices: none -> 21.2 us  [doubled_up(): theirs = lax.ppermute(grown, axis, [(d, d ^ reach) for d in range(ways)])]
    ppermute x0 -> x2, starting transfers between devices: none -> 3.5 us  [doubled_up(): theirs = lax.ppermute(grown, axis, [(d, d ^ reach) for d in range(ways)])]
  transfers between devices with their start and end apart: 8 -> 9, of which waited for: 6 -> 7; matrix products, arithmetic and copies ran while one was open for 2% -> 2% of each run, Pallas kernels for 0% -> 0%
where the time goes in v1:
time: 268 us
  waiting for transfers between devices  173 us (65%)
  matrix products  39.4 us (15%)
  starting transfers between devices  23.1 us (9%)
  between operations  14.8 us (6%)
  local copies, waits for them, and re-layouts  10.3 us (4%)
  other arithmetic  7 us (3%)
    psum x1, waiting for transfers between devices, shards(): grad_in, grad_out = lax.psum((local_in, local_out), ('dp', 'tm', 'space'))  139 us
    dot_general x54, matrix products, causal_conv(): jnp.dot(window.reshape(-1, channels), weight[tap_time, tap_row, tap_col],...  28.1 us
    ppermute x2, waiting for transfers between devices, doubled_up(): theirs = lax.ppermute(grown, axis, [(d, d ^ reach) for d in range(ways)])  21.2 us
    ppermute x2, waiting for transfers between devices, from_behind(): return lax.ppermute(value, axis, pairs)  9 us
    ppermute x2, starting transfers between devices, extended_2(): lax.ppermute(lax.slice_in_dim(block, block.shape[dim] - width, None, axis...  8.42 us
    ppermute x2, starting transfers between devices, from_behind(): return lax.ppermute(value, axis, pairs)  8.39 us
    slice x5, local copies, waits for them, and re-layouts, causal_conv(): extended[tap_time:tap_time + frame_count, tap_row:tap_row + row_count, ta...  5.87 us
  transfers between devices with their start and end apart: 9, of which 7 were waited for; matrix products, arithmetic and copies ran while one was open for 2% of the time, Pallas kernels for 0%

profile of v1, /device:TPU:0, one launch (start us, length us, event | category | flops | bytes accessed | tf_op | source)
XLA Modules:
  0.0 267.8 jit_solution(14751571623170421748)
XLA Ops:
  7.2 1.2 multiply_reduce_fusion.2
  8.6 1.2 multiply_convert_fusion.3
  9.8 0.6 collective-permute-start
  10.4 1.5 collective-permute-done
  12.2 2.9 %collective-permute-start.1 = (bf16[3,416,384]{2,1,0:T(8,128)(2,1)S(1)}, bf16[3,416,384]{2,1,0:T(8,128)(2,1)S(1)}, u32[]{:S(2)}, u32[]{:S(2)}) collective-permute-start(bf16[3,416,384]{2,1,0:T(8,128)(2,1)S(1)} %maximum_select_fusion.1), channel_id=1, source_target_pairs={{0,2},{1,3},{2,0},{3,1},{4,6},{5,7},{6,4},{7,5},{8,10},{9,11},{10,... | collective-permute-start | bytes 2875400 | tf_op jit(solution)/shard_map/ppermute | solution.py:11
  15.2 1.7 convolution_convert_fusion.2
  16.9 19.8 %collective-permute-done.1 = bf16[3,416,384]{2,1,0:T(8,128)(2,1)S(1)} collective-permute-done((bf16[3,416,384]{2,1,0:T(8,128)(2,1)S(1)}, bf16[3,416,384]{2,1,0:T(8,128)(2,1)S(1)}, u32[]{:S(2)}, u32[]{:S(2)}) %collective-permute-start.1) | collective-permute-done | bytes 958496 | tf_op jit(solution)/shard_map/ppermute | solution.py:11
  37.1 1.3 convolution_convert_fusion.1
  38.5 1.3 convolution_convert_fusion
  39.8 1.1 multiply_reduce_fusion
  40.9 0.6 fusion.1
  41.5 1.0 fusion.47
  42.6 0.6 fusion.54
  43.6 3.7 %collective-permute-start.2 = (bf16[2,2,104,384]{3,2,1,0:T(8,128)(2,1)S(1)}, bf16[2,2,104,384]{3,2,1,0:T(8,128)(2,1)S(1)}, u32[]{:S(2)}, u32[]{:S(2)}) collective-permute-start(bf16[2,2,104,384]{3,2,1,0:T(8,128)(2,1)S(1)} %bitcast.381), channel_id=1, source_target_pairs={{0,4},{4,8},{8,12},{1,5},{5,9},{9,13},{2,6},{6,10},{10,14},{3,7},{... | collective-permute-start | bytes 958472 | tf_op jit(solution)/shard_map/ppermute | solution.py:22
  47.8 5.7 %collective-permute-done.2 = bf16[2,2,104,384]{3,2,1,0:T(8,128)(2,1)S(1)} collective-permute-done((bf16[2,2,104,384]{3,2,1,0:T(8,128)(2,1)S(1)}, bf16[2,2,104,384]{3,2,1,0:T(8,128)(2,1)S(1)}, u32[]{:S(2)}, u32[]{:S(2)}) %collective-permute-start.2) | collective-permute-done | bytes 319520 | tf_op jit(solution)/shard_map/ppermute | solution.py:22
  53.6 1.3 collective-permute-start.3
  55.0 1.5 collective-permute-start.4
  57.6 2.7 %collective-permute-done.4 = bf16[5,1,104,384]{3,2,1,0:T(8,128)(2,1)S(1)} collective-permute-done((bf16[5,1,104,384]{3,2,1,0:T(8,128)(2,1)S(1)}, bf16[5,1,104,384]{3,2,1,0:T(8,128)(2,1)S(1)}, u32[]{:S(2)}, u32[]{:S(2)}) %collective-permute-start.4) | collective-permute-done | bytes 399392 | tf_op jit(solution)/shard_map/ppermute | solution.py:33
  60.3 0.7 fusion.10
  61.0 2.6 fusion.226
  72.6 0.7 fusion.44
  73.4 0.5 fusion.42
  73.9 0.7 fusion.40
  74.6 0.5 fusion.35
  75.1 0.6 fusion.33
  75.7 0.5 fusion.31
  76.3 0.6 multiply_reduce_fusion.1
  77.3 4.7 %collective-permute-start.5 = (bf16[2,2,104,384]{3,2,1,0:T(8,128)(2,1)S(1)}, bf16[2,2,104,384]{3,2,1,0:T(8,128)(2,1)S(1)}, u32[]{:S(2)}, u32[]{:S(2)}) collective-permute-start(bf16[2,2,104,384]{3,2,1,0:T(8,128)(2,1)S(1)} %bitcast.380), channel_id=1, source_target_pairs={{0,4},{4,8},{8,12},{1,5},{5,9},{9,13},{2,6},{6,10},{10,14},{3,7},{... | collective-permute-start | bytes 958472 | tf_op jit(solution)/shard_map/ppermute | solution.py:22
  82.0 0.6 multiply_convert_fusion.1
  83.1 3.3 %collective-permute-done.5 = bf16[2,2,104,384]{3,2,1,0:T(8,128)(2,1)S(1)} collective-permute-done((bf16[2,2,104,384]{3,2,1,0:T(8,128)(2,1)S(1)}, bf16[2,2,104,384]{3,2,1,0:T(8,128)(2,1)S(1)}, u32[]{:S(2)}, u32[]{:S(2)}) %collective-permute-start.5) | collective-permute-done | bytes 319520 | tf_op jit(solution)/shard_map/ppermute | solution.py:22
  86.5 7.1 %collective-permute-start.6 = (bf16[5,1,104,384]{3,2,1,0:T(8,128)(2,1)S(1)}, bf16[5,1,104,384]{3,2,1,0:T(8,128)(2,1)S(1)}, u32[]{:S(2)}, u32[]{:S(2)}) collective-permute-start(bf16[5,1,104,384]{3,2,1,0:T(8,128)(2,1)S(1)} %get-tuple-element.60), channel_id=1, source_target_pairs={{0,1},{1,2},{2,3},{4,5},{5,6},{6,7},{8,9},{9,10},{10,11},{12,13},{... | collective-permute-start | bytes 1198088 | tf_op jit(solution)/shard_map/ppermute | solution.py:30
  93.6 1.3 collective-permute-start.7
  96.1 1.4 collective-permute-done.7
  97.5 0.7 select_maximum_fusion
  98.2 2.8 %fusion.225 = (bf16[3,2,104,384]{3,2,1,0:T(8,128)(2,1)S(1)}, bf16[3,2,104,384]{3,2,1,0:T(8,128)(2,1)S(1)}, bf16[3,2,104,384]{3,2,1,0:T(8,128)(2,1)S(1)}, bf16[3,...) fusion(bf16[5,4,106,384]{3,2,1,0:T(8,128)(2,1)S(1)} %select_max, ...), kind=kLoop, calls=%fused_computation.285 | loop fusion | bytes 17252352 | tf_op jit(solution)/shard_map/slice | solution.py:64
  110.0 0.8 fusion.29
  110.8 0.5 fusion.27
  111.4 0.7 fusion.25
  112.0 0.6 fusion.20
  112.6 0.6 fusion.18
  113.2 0.5 fusion.16
  113.7 0.5 fusion.48
  114.2 0.7 multiply_convert_fusion
  114.9 1.3 fusion.231
  116.2 1.8 convolution_bitcast_fusion
  118.1 138.9 %all-reduce.5.cloned.1.call-done = (f32[384,384]{0,1:T(8,128)}, f32[384,384]{1,0:T(8,128)}) async-done(((f32[384,384]{0,1:T(8,128)}, f32[384,384]{1,0:T(8,128)}), (f32[384,384]{0,1:T(8,128)}, f32[384,384]{1,0:T(8,128)})) %all-reduce.5.cloned.1.call-update) | async-done | bytes 1179664 | tf_op jit(solution)/shard_map/psum | solution.py:147
  257.0 2.1 copy.15
  259.1 1.9 copy.18
  (94 shorter events, 23.3 us)
Async XLA Ops:
  7.2 30.0 %copy-start = (bf16[384,384]{1,0:T(8,128)(2,1)S(1)}, bf16[384,384]{1,0:T(8,128)(2,1)}, u32[]{:S(2)}) copy-start(bf16[384,384]{1,0:T(8,128)(2,1)} %param.15) | copy-start | bytes 884740
  7.2 249.8 %all-reduce.5.cloned.1.call-start = ((), (), s32[]{:S(2)}) async-start(), calls=%async_computation | async-start | bytes 2359296 | tf_op jit(solution)/shard_map/psum | solution.py:147
  9.8 2.0 collective-permute-start
  12.2 24.5 %collective-permute-start.1 = (bf16[3,416,384]{2,1,0:T(8,128)(2,1)S(1)}, bf16[3,416,384]{2,1,0:T(8,128)(2,1)S(1)}, u32[]{:S(2)}, u32[]{:S(2)}) collective-permute-start(bf16[3,416,384]{2,1,0:T(8,128)(2,1)S(1)} %maximum_select_fusion.1), channel_id=1, source_target_pairs={{0,2},{1,3},{2,0},{3,1},{4,6},{5,7},{6,4},{7,5},{8,10},{9,11},{10,... | collective-permute-start | bytes 2875400 | tf_op jit(solution)/shard_map/ppermute | solution.py:11
  37.1 1.4 copy-start.4
  39.8 7.5 %slice-start = ((s8[7962624]{0:T(1024)(128)(4,1)}), s8[4194304]{0:T(1024)(128)(4,1)S(1)}, s32[]{:S(2)}) async-start(s8[7962624]{0:T(1024)(128)(4,1)} %bitcast.315), calls=%async_computation.1 | async-start | bytes 8388608
  41.5 1.0 copy-start.2
  41.5 1.1 copy-start.7
  41.5 1.7 copy-start.5
  41.5 5.8 %slice-start.1 = ((s8[7962624]{0:T(1024)(128)(4,1)}), s8[3768320]{0:T(1024)(128)(4,1)S(1)}, s32[]{:S(2)}) async-start(s8[7962624]{0:T(1024)(128)(4,1)} %bitcast.315), calls=%async_computation.2 | async-start | bytes 7536640
  43.6 9.9 %collective-permute-start.2 = (bf16[2,2,104,384]{3,2,1,0:T(8,128)(2,1)S(1)}, bf16[2,2,104,384]{3,2,1,0:T(8,128)(2,1)S(1)}, u32[]{:S(2)}, u32[]{:S(2)}) collective-permute-start(bf16[2,2,104,384]{3,2,1,0:T(8,128)(2,1)S(1)} %bitcast.381), channel_id=1, source_target_pairs={{0,4},{4,8},{8,12},{1,5},{5,9},{9,13},{2,6},{6,10},{10,14},{3,7},{... | collective-permute-start | bytes 958472 | tf_op jit(solution)/shard_map/ppermute | solution.py:22
  53.6 3.9 %collective-permute-start.3 = (bf16[5,1,104,384]{3,2,1,0:T(8,128)(2,1)S(1)}, bf16[5,1,104,384]{3,2,1,0:T(8,128)(2,1)S(1)}, u32[]{:S(2)}, u32[]{:S(2)}) collective-permute-start(bf16[5,1,104,384]{3,2,1,0:T(8,128)(2,1)S(1)} %get-tuple-element.66), channel_id=1, source_target_pairs={{0,1},{1,2},{2,3},{4,5},{5,6},{6,7},{8,9},{9,10},{10,11},{12,13},{... | collective-permute-start | bytes 1198088 | tf_op jit(solution)/shard_map/ppermute | solution.py:30
  55.0 5.3 %collective-permute-start.4 = (bf16[5,1,104,384]{3,2,1,0:T(8,128)(2,1)S(1)}, bf16[5,1,104,384]{3,2,1,0:T(8,128)(2,1)S(1)}, u32[]{:S(2)}, u32[]{:S(2)}) collective-permute-start(bf16[5,1,104,384]{3,2,1,0:T(8,128)(2,1)S(1)} %get-tuple-element.67), channel_id=1, source_target_pairs={{1,0},{2,1},{3,2},{5,4},{6,5},{7,6},{9,8},{10,9},{11,10},{13,12},{... | collective-permute-start | bytes 1198088 | tf_op jit(solution)/shard_map/ppermute | solution.py:33
  75.7 1.2 copy-start.6
  75.7 6.9 %slice-start.2 = ((s8[7962624]{0:T(1024)(128)(4,1)}), s8[4194304]{0:T(1024)(128)(4,1)S(1)}, s32[]{:S(2)}) async-start(s8[7962624]{0:T(1024)(128)(4,1)} %bitcast.317), calls=%async_computation.3 | async-start | bytes 8388608
  76.3 5.7 %copy-start.8 = (bf16[384,384]{1,0:T(8,128)(2,1)S(1)}, bf16[384,384]{1,0:T(8,128)(2,1)}, u32[]{:S(2)}) copy-start(bf16[384,384]{1,0:T(8,128)(2,1)} %param.22) | copy-start | bytes 884740
  76.3 6.3 %slice-start.3 = ((s8[7962624]{0:T(1024)(128)(4,1)}), s8[3768320]{0:T(1024)(128)(4,1)S(1)}, s32[]{:S(2)}) async-start(s8[7962624]{0:T(1024)(128)(4,1)} %bitcast.317), calls=%async_computation.4 | async-start | bytes 7536640
  77.3 9.1 %collective-permute-start.5 = (bf16[2,2,104,384]{3,2,1,0:T(8,128)(2,1)S(1)}, bf16[2,2,104,384]{3,2,1,0:T(8,128)(2,1)S(1)}, u32[]{:S(2)}, u32[]{:S(2)}) collective-permute-start(bf16[2,2,104,384]{3,2,1,0:T(8,128)(2,1)S(1)} %bitcast.380), channel_id=1, source_target_pairs={{0,4},{4,8},{8,12},{1,5},{5,9},{9,13},{2,6},{6,10},{10,14},{3,7},{... | collective-permute-start | bytes 958472 | tf_op jit(solution)/shard_map/ppermute | solution.py:22
  86.5 9.5 %collective-permute-start.6 = (bf16[5,1,104,384]{3,2,1,0:T(8,128)(2,1)S(1)}, bf16[5,1,104,384]{3,2,1,0:T(8,128)(2,1)S(1)}, u32[]{:S(2)}, u32[]{:S(2)}) collective-permute-start(bf16[5,1,104,384]{3,2,1,0:T(8,128)(2,1)S(1)} %get-tuple-element.60), channel_id=1, source_target_pairs={{0,1},{1,2},{2,3},{4,5},{5,6},{6,7},{8,9},{9,10},{10,11},{12,13},{... | collective-permute-start | bytes 1198088 | tf_op jit(solution)/shard_map/ppermute | solution.py:30
  93.6 3.8 %collective-permute-start.7 = (bf16[5,1,104,384]{3,2,1,0:T(8,128)(2,1)S(1)}, bf16[5,1,104,384]{3,2,1,0:T(8,128)(2,1)S(1)}, u32[]{:S(2)}, u32[]{:S(2)}) collective-permute-start(bf16[5,1,104,384]{3,2,1,0:T(8,128)(2,1)S(1)} %get-tuple-element.61), channel_id=1, source_target_pairs={{1,0},{2,1},{3,2},{5,4},{6,5},{7,6},{9,8},{10,9},{11,10},{13,12},{... | collective-permute-start | bytes 1198088 | tf_op jit(solution)/shard_map/ppermute | solution.py:33
  113.2 1.1 copy-start.9
  114.2 3.8 %copy-start.3 = (bf16[624,384]{1,0:T(8,128)(2,1)}, bf16[624,384]{1,0:T(8,128)(2,1)S(1)}, u32[]{:S(2)}) copy-start(bf16[624,384]{1,0:T(8,128)(2,1)S(1)} %fusion.48) | copy-start | bytes 1437700
  116.2 144.8 %copy-start.1 = (bf16[384,384]{1,0:T(8,128)(2,1)S(1)}, bf16[384,384]{1,0:T(8,128)(2,1)}, u32[]{:S(2)}) copy-start(bf16[384,384]{1,0:T(8,128)(2,1)} %param.15) | copy-start | bytes 884740
Sparse Core Ops, SparseCore 0:
  118.2 138.7 all-reduce.4
